TPU v7x, 32 devices: a whole 2x2x4 slice. The times are simulated.
32 devices in a mesh: groups: 2 (over x), tm: 16 (over z, y, core).
Axes of the slice: x: 2, y: 2, z: 4, core: 2. Of those that a mesh axis runs over, the one named last changes fastest.
Arguments:
- latent: bfloat16 [64, 8192], P('groups', 'tm'), parts along dimension 0, may hold values from -6 to 6
- w_in: bfloat16 [3, 3, 3, 16, 384], replicated, may hold values from -0.3125 to 0.3125
- b_in: float32 [384], replicated, may hold values from -3 to 3
- gain: float32 [384], replicated, may hold values from 0.1 to 1.9
- w_mid: bfloat16 [3, 3, 3, 384, 384], replicated, may hold values from -0.0625 to 0.0625
- b_mid: float32 [384], replicated, may hold values from -3 to 3
- w_time: bfloat16 [3, 384, 768], replicated, may hold values from -0.1875 to 0.1875
- b_time: float32 [768], replicated, may hold values from -3 to 3
Outputs:
- frames_up: bfloat16 [128, 16, 32, 384], P(('groups', 'tm')), parts along dimension 0
There are 2 independent parts, one for each index of `groups`. A program takes and returns all parts, laid end to end along the dimension named above; an argument that names none is the same for every part. Nothing has to cross between parts.
All inputs are finite; a program needn't handle non-finite values.
Results may differ from a plain program's by a relative error of at most 0.012.
Values may be sent and summed in bfloat16 or wider, within the bound.
A program may use at most 128 MiB of HBM per device.

v0:
```python
import jax
import jax.numpy as jnp
from jax import lax
from jax.sharding import PartitionSpec as P

ZC = 16
C = 384
H = 16
W = 32


def passed_along(block, axis, distance):
    devices = range(lax.axis_size(axis))
    route = [(i - distance, i) for i in devices if i - distance in devices]
    return lax.ppermute(block, axis, route)


def conv_valid(padded, weight, bias, spatial):
    frames = padded.shape[0] - 2
    rows = padded.shape[1]
    inner = padded.shape[3]
    if spatial:
        margin = 1
        padded = jnp.pad(padded, ((0, 0), (1, 1), (margin, margin), (0, 0)))
        taps = 3
    else:
        taps = 1
    cols = padded.shape[2] - taps + 1
    total = jnp.zeros((frames * rows * cols, weight.shape[-1]), jnp.float32)
    for step_t in range(3):
        for step_h in range(taps):
            for step_w in range(taps):
                window = padded[
                    step_t : step_t + frames, step_h : step_h + rows, step_w : step_w + cols, :
                ]
                if spatial:
                    kernel = weight[step_t, step_h, step_w]
                else:
                    kernel = weight[step_t]
                total = total + jnp.dot(
                    window.reshape(-1, inner), kernel, preferred_element_type=jnp.float32
                )
    return (total + bias).reshape(frames, rows, cols, weight.shape[-1])


def conv_input(padded, weight, bias):
    frames = padded.shape[0] - 2
    rows = padded.shape[1]
    inner = padded.shape[3]
    margin = 1
    padded = jnp.pad(padded, ((0, 0), (1, 1), (margin, margin), (0, 0)))
    cols = padded.shape[2] - 2
    windows = []
    for step_t in range(3):
        for step_h in range(3):
            for step_w in range(3):
                windows.append(
                    padded[
                        step_t : step_t + frames, step_h : step_h + rows, step_w : step_w + cols, :
                    ]
                )
    stacked = jnp.concatenate(windows, axis=-1).reshape(frames * rows * cols, 27 * inner)
    total = jnp.dot(
        stacked, weight.reshape(27 * inner, weight.shape[-1]), preferred_element_type=jnp.float32
    )
    return (total + bias).reshape(frames, rows, cols, weight.shape[-1])


def activate(hidden, gain):
    values = hidden.astype(jnp.float32)
    scale = lax.rsqrt(jnp.mean(values * values, axis=-1, keepdims=True) + 1e-06)
    return jax.nn.silu(values * scale * gain).astype(jnp.bfloat16)


def per_device(latent, w_in, b_in, gain, w_mid, b_mid, w_time, b_time):
    owned = lax.all_to_all(latent, "tm", split_axis=0, concat_axis=1, tiled=True)
    frames = owned.shape[0]
    lat = owned.reshape(frames, H, W, ZC)
    earlier = passed_along(lat, "tm", 1)
    h0 = conv_input(jnp.concatenate([earlier, lat], axis=0), w_in, b_in).astype(jnp.bfloat16)
    act = activate(h0, gain)
    earlier_act = passed_along(act, "tm", 1)
    branch = conv_valid(jnp.concatenate([earlier_act, act], axis=0), w_mid, b_mid, True)
    h1 = (h0.astype(jnp.float32) + branch).astype(jnp.bfloat16)
    earlier_block = passed_along(h1, "tm", 1)
    up = conv_valid(jnp.concatenate([earlier_block, h1], axis=0), w_time, b_time, False)
    paired = up.reshape(frames, H, W, 2, C).transpose(0, 3, 1, 2, 4)
    return paired.reshape(2 * frames, H, W, C).astype(jnp.bfloat16)


def solution(mesh):
    return jax.shard_map(
        per_device,
        mesh=mesh,
        in_specs=(P("groups", "tm"), P(), P(), P(), P(), P(), P(), P()),
        out_specs=P(("groups", "tm"), None, None, None),
        check_vma=False,
    )
```

profile of v0, /device:TPU:8, one launch (start us, length us, event | category | flops | bytes accessed | tf_op | source)
XLA Modules:
  0.0 154.6 jit_solution(9824151615422119328)
XLA Ops:
  0.0 0.8 all_to_all.12
  0.8 11.1 %all_to_all.16 = bf16[16,2,512]{2,1,0:T(2,128)(2,1)S(1)} all-to-all(bf16[16,2,512]{2,1,0:T(2,128)(2,1)S(1)} %all_to_all.12), channel_id=1, replica_groups=mesh['groups'=2,'tm'=16] {'tm'}, dimensions={0} | all-to-all | bytes 65536 | tf_op jit(solution)/shard_map/all_to_all | solution.py:76
  12.2 2.0 %collective-permute-start = (bf16[2,16,32,16]{3,2,1,0:T(8,128)(2,1)S(1)}, bf16[2,16,32,16]{3,2,1,0:T(8,128)(2,1)S(1)}, u32[]{:S(2)}, u32[]{:S(2)}) collective-permute-start(bf16[2,16,32,16]{3,2,1,0:T(8,128)(2,1)S(1)} %reshape.157), channel_id=1, source_target_pairs={{0,1},{1,2},{2,3},{3,4},{4,5},{5,6},{6,7},{7,8},{8,9},{9,10},{10,1... | collective-permute-start | bytes 98312 | tf_op jit(solution)/shard_map/ppermute | solution.py:15
  14.6 6.2 %collective-permute-done = bf16[2,16,32,16]{3,2,1,0:T(8,128)(2,1)S(1)} collective-permute-done((bf16[2,16,32,16]{3,2,1,0:T(8,128)(2,1)S(1)}, bf16[2,16,32,16]{3,2,1,0:T(8,128)(2,1)S(1)}, u32[]{:S(2)}, u32[]{:S(2)}) %collective-permute-start) | collective-permute-done | bytes 32800 | tf_op jit(solution)/shard_map/ppermute | solution.py:15
  21.2 2.5 %pad_slice_fusion.26 = (bf16[2,16,32,16]{3,2,1,0:T(8,128)(2,1)}, bf16[2,16,32,16]{3,2,1,0:T(8,128)(2,1)}, bf16[2,16,32,16]{3,2,1,0:T(8,128)(2,1)}, bf16[2,16,32,...) fusion(bf16[4,16,32,16]{3,2,1,0:T(8,128)(2,1)S(1)} %constant_dy, ...), kind=kLoop, calls=%fused_computation.36 | loop fusion | bytes 688128 | tf_op jit(solution)/shard_map/slice | solution.py:58
  24.6 0.7 copy.90
  25.3 0.7 copy.91
  26.0 0.7 copy.92
  28.3 1.7 %copy.94 = bf16[1024,16]{0,1:T(8,128)(2,1)} copy(bf16[1024,16]{1,0:T(8,128)(2,1)} %bitcast.240) | data formatting | bytes 65536 | tf_op jit(solution)/shard_map/concatenate | solution.py:62
  30.0 1.7 %copy.70 = bf16[1024,16]{0,1:T(8,128)(2,1)} copy(bf16[1024,16]{1,0:T(8,128)(2,1)} %bitcast.239) | data formatting | bytes 65536 | tf_op jit(solution)/shard_map/concatenate | solution.py:62
  31.7 1.7 %copy.71 = bf16[1024,16]{0,1:T(8,128)(2,1)} copy(bf16[1024,16]{1,0:T(8,128)(2,1)} %bitcast.238) | data formatting | bytes 65536 | tf_op jit(solution)/shard_map/concatenate | solution.py:62
  33.4 1.7 %copy.72 = bf16[1024,16]{0,1:T(8,128)(2,1)} copy(bf16[1024,16]{1,0:T(8,128)(2,1)} %bitcast.237) | data formatting | bytes 65536 | tf_op jit(solution)/shard_map/concatenate | solution.py:62
  35.1 1.7 %copy.74 = bf16[1024,16]{0,1:T(8,128)(2,1)} copy(bf16[1024,16]{1,0:T(8,128)(2,1)} %bitcast.236) | data formatting | bytes 65536 | tf_op jit(solution)/shard_map/concatenate | solution.py:62
  36.7 1.7 %copy.75 = bf16[1024,16]{0,1:T(8,128)(2,1)} copy(bf16[1024,16]{1,0:T(8,128)(2,1)} %bitcast.235) | data formatting | bytes 65536 | tf_op jit(solution)/shard_map/concatenate | solution.py:62
  38.4 1.7 %copy.76 = bf16[1024,16]{0,1:T(8,128)(2,1)} copy(bf16[1024,16]{1,0:T(8,128)(2,1)} %bitcast.234) | data formatting | bytes 65536 | tf_op jit(solution)/shard_map/concatenate | solution.py:62
  40.1 0.7 copy.77
  58.4 2.0 %multiply_reduce_fusion = (f32[1024]{0:T(1024)S(1)}, f32[1024,384]{1,0:T(8,128)S(1)}) fusion(f32[384]{0:T(512)S(1)} %copy-done.44, bf16[1024,432]{0,1:T(8,128)(2,1)} %constant_dynamic-update-slice_fusion.2, bf16[432,384]{1,0:T(8,128)(2,1)S(1)} %bitcast.180), kind=kOutput, calls=%fused_computation.33 | convolution fusion | flops 341703680 | bytes 2795008 | tf_op jit(solution)/shard_map/dot_general | solution.py:63
  61.0 1.9 %collective-permute-start.1 = (bf16[2,16,32,384]{3,2,1,0:T(8,128)(2,1)S(1)}, bf16[2,16,32,384]{3,2,1,0:T(8,128)(2,1)S(1)}, u32[]{:S(2)}, u32[]{:S(2)}) collective-permute-start(bf16[2,16,32,384]{3,2,1,0:T(8,128)(2,1)S(1)} %multiply_convert_fusion.1), channel_id=1, source_target_pairs={{0,1},{1,2},{2,3},{3,4},{4,5},{5,6},{6,7},{7,8},{8,9},{9,10},{10,1... | collective-permute-start | bytes 2359304 | tf_op jit(solution)/shard_map/ppermute | solution.py:15
  62.9 3.0 %fusion.3 = f32[1024,384]{1,0:T(8,128)} fusion(f32[1024,384]{1,0:T(8,128)S(1)} %get-tuple-element.55, f32[384]{0:T(512)S(1)} %copy-done.43, f32[1024]{0:T(1024)S(1)} %add_rsqrt_fusion, bf16[3,3,3,384,384]{4,3,2,1,0:T(8,128)(2,1)} %param.12), kind=kOutput, calls=%fused_computation.63 | convolution fusion | flops 304742400 | bytes 3446272 | tf_op jit(solution)/shard_map/dot_general | solution.py:40
  65.9 9.3 %collective-permute-done.1 = bf16[2,16,32,384]{3,2,1,0:T(8,128)(2,1)S(1)} collective-permute-done((bf16[2,16,32,384]{3,2,1,0:T(8,128)(2,1)S(1)}, bf16[2,16,32,384]{3,2,1,0:T(8,128)(2,1)S(1)}, u32[]{:S(2)}, u32[]{:S(2)}) %collective-permute-start.1) | collective-permute-done | bytes 786464 | tf_op jit(solution)/shard_map/ppermute | solution.py:15
  75.4 2.1 %pad_slice_fusion.23 = (bf16[2,16,32,384]{3,2,1,0:T(8,128)(2,1)S(1)}, bf16[2,16,32,384]{3,2,1,0:T(8,128)(2,1)S(1)}, bf16[2,16,32,384]{3,2,1,0:T(8,128)(2,1)S(1)}...) fusion(bf16[4,16,32,384]{3,2,1,0:T(8,128)(2,1)S(1)} %pad_maximum_fusion), kind=kLoop, calls=%fused_computation.23 | loop fusion | bytes 5505024 | tf_op jit(solution)/shard_map/slice | solution.py:33
  77.5 6.2 %pad_slice_fusion = (bf16[2,16,32,384]{3,2,1,0:T(8,128)(2,1)}, bf16[2,16,32,384]{3,2,1,0:T(8,128)(2,1)}, bf16[2,16,32,384]{3,2,1,0:T(8,128)(2,1)}, bf16[2,16,32,...) fusion(bf16[4,16,32,384]{3,2,1,0:T(8,128)(2,1)S(1)} %pad_maximu, ...), kind=kLoop, calls=%fused_computation | loop fusion | bytes 16515072 | tf_op jit(solution)/shard_map/slice | solution.py:33
  88.3 1.8 %fusion.12 = f32[1024,384]{1,0:T(8,128)} fusion(bf16[1024,384]{1,0:T(8,128)(2,1)S(1)} %bitcast.210, bf16[3,3,3,384,384]{4,3,2,1,0:T(8,128)(2,1)S(1)} %bitcast.185), kind=kOutput, calls=%fused_computation.72 | convolution fusion | flops 301989888 | bytes 2654208 | tf_op jit(solution)/shard_map/dot_general | solution.py:40
  90.0 1.8 %fusion.59 = f32[1024,384]{1,0:T(8,128)} fusion(bf16[1024,384]{1,0:T(8,128)(2,1)S(1)} %bitcast.205, bf16[3,3,3,384,384]{4,3,2,1,0:T(8,128)(2,1)S(1)} %bitcast.185), kind=kOutput, calls=%fused_computation.119 | convolution fusion | flops 301989888 | bytes 2654208 | tf_op jit(solution)/shard_map/dot_general | solution.py:40
  91.8 1.8 %fusion.57 = f32[1024,384]{1,0:T(8,128)} fusion(bf16[1024,384]{1,0:T(8,128)(2,1)S(1)} %bitcast.204, bf16[3,3,3,384,384]{4,3,2,1,0:T(8,128)(2,1)S(1)} %bitcast.185), kind=kOutput, calls=%fused_computation.117 | convolution fusion | flops 301989888 | bytes 2654208 | tf_op jit(solution)/shard_map/dot_general | solution.py:40
  93.6 1.8 %fusion.55 = f32[1024,384]{1,0:T(8,128)} fusion(bf16[1024,384]{1,0:T(8,128)(2,1)S(1)} %bitcast.203, bf16[3,3,3,384,384]{4,3,2,1,0:T(8,128)(2,1)S(1)} %bitcast.185), kind=kOutput, calls=%fused_computation.115 | convolution fusion | flops 301989888 | bytes 2654208 | tf_op jit(solution)/shard_map/dot_general | solution.py:40
  95.4 1.8 %fusion.51 = f32[1024,384]{1,0:T(8,128)} fusion(bf16[1024,384]{1,0:T(8,128)(2,1)S(1)} %bitcast.202, bf16[3,3,3,384,384]{4,3,2,1,0:T(8,128)(2,1)S(1)} %bitcast.185), kind=kOutput, calls=%fused_computation.111 | convolution fusion | flops 301989888 | bytes 2654208 | tf_op jit(solution)/shard_map/dot_general | solution.py:40
  97.2 1.8 %fusion.49 = f32[1024,384]{1,0:T(8,128)} fusion(bf16[1024,384]{1,0:T(8,128)(2,1)S(1)} %bitcast.201, bf16[3,3,3,384,384]{4,3,2,1,0:T(8,128)(2,1)S(1)} %bitcast.185), kind=kOutput, calls=%fused_computation.109 | convolution fusion | flops 301989888 | bytes 2654208 | tf_op jit(solution)/shard_map/dot_general | solution.py:40
  99.1 1.8 %fusion.47 = f32[1024,384]{1,0:T(8,128)} fusion(bf16[1024,384]{1,0:T(8,128)(2,1)S(1)} %bitcast.200, bf16[3,3,3,384,384]{4,3,2,1,0:T(8,128)(2,1)S(1)} %bitcast.185), kind=kOutput, calls=%fused_computation.107 | convolution fusion | flops 301989888 | bytes 2654208 | tf_op jit(solution)/shard_map/dot_general | solution.py:40
  100.9 1.9 %fusion.45 = f32[1024,384]{1,0:T(8,128)} fusion(bf16[1024,384]{1,0:T(8,128)(2,1)S(1)} %bitcast.199, bf16[3,3,3,384,384]{4,3,2,1,0:T(8,128)(2,1)S(1)} %bitcast.185), kind=kOutput, calls=%fused_computation.105 | convolution fusion | flops 301989888 | bytes 2654208 | tf_op jit(solution)/shard_map/dot_general | solution.py:40
  102.7 1.8 %fusion.43 = f32[1024,384]{1,0:T(8,128)} fusion(bf16[1024,384]{1,0:T(8,128)(2,1)S(1)} %bitcast.198, bf16[3,3,3,384,384]{4,3,2,1,0:T(8,128)(2,1)S(1)} %bitcast.185), kind=kOutput, calls=%fused_computation.103 | convolution fusion | flops 301989888 | bytes 2654208 | tf_op jit(solution)/shard_map/dot_general | solution.py:40
  104.5 1.8 %fusion.41 = f32[1024,384]{1,0:T(8,128)} fusion(bf16[1024,384]{1,0:T(8,128)(2,1)S(1)} %bitcast.197, bf16[3,3,3,384,384]{4,3,2,1,0:T(8,128)(2,1)S(1)} %bitcast.185), kind=kOutput, calls=%fused_computation.101 | convolution fusion | flops 301989888 | bytes 2654208 | tf_op jit(solution)/shard_map/dot_general | solution.py:40
  106.3 1.8 %fusion.39 = f32[1024,384]{1,0:T(8,128)} fusion(bf16[1024,384]{1,0:T(8,128)(2,1)S(1)} %bitcast.196, bf16[3,3,3,384,384]{4,3,2,1,0:T(8,128)(2,1)S(1)} %bitcast.185), kind=kOutput, calls=%fused_computation.99 | convolution fusion | flops 301989888 | bytes 2654208 | tf_op jit(solution)/shard_map/dot_general | solution.py:40
  108.1 1.8 %fusion.37 = f32[1024,384]{1,0:T(8,128)} fusion(bf16[1024,384]{1,0:T(8,128)(2,1)S(1)} %bitcast.195, bf16[3,3,3,384,384]{4,3,2,1,0:T(8,128)(2,1)S(1)} %bitcast.185), kind=kOutput, calls=%fused_computation.97 | convolution fusion | flops 301989888 | bytes 2654208 | tf_op jit(solution)/shard_map/dot_general | solution.py:40
  109.9 1.8 %fusion.33 = f32[1024,384]{1,0:T(8,128)} fusion(bf16[1024,384]{1,0:T(8,128)(2,1)S(1)} %bitcast.194, bf16[3,3,3,384,384]{4,3,2,1,0:T(8,128)(2,1)S(1)} %bitcast.185), kind=kOutput, calls=%fused_computation.93 | convolution fusion | flops 301989888 | bytes 2654208 | tf_op jit(solution)/shard_map/dot_general | solution.py:40
  111.6 1.8 %fusion.31 = f32[1024,384]{1,0:T(8,128)} fusion(bf16[1024,384]{1,0:T(8,128)(2,1)S(1)} %bitcast.193, bf16[3,3,3,384,384]{4,3,2,1,0:T(8,128)(2,1)S(1)} %bitcast.185), kind=kOutput, calls=%fused_computation.91 | convolution fusion | flops 301989888 | bytes 2654208 | tf_op jit(solution)/shard_map/dot_general | solution.py:40
  113.5 2.1 %fusion.29 = f32[1024,384]{1,0:T(8,128)} fusion(bf16[1024,384]{1,0:T(8,128)(2,1)S(1)} %bitcast.192, bf16[3,3,3,384,384]{4,3,2,1,0:T(8,128)(2,1)S(1)} %bitcast.185), kind=kOutput, calls=%fused_computation.89 | convolution fusion | flops 301989888 | bytes 2654208 | tf_op jit(solution)/shard_map/dot_general | solution.py:40
  115.5 1.9 %fusion.27 = f32[1024,384]{1,0:T(8,128)} fusion(bf16[1024,384]{1,0:T(8,128)(2,1)S(1)} %bitcast.191, bf16[3,3,3,384,384]{4,3,2,1,0:T(8,128)(2,1)S(1)} %bitcast.185), kind=kOutput, calls=%fused_computation.87 | convolution fusion | flops 301989888 | bytes 2654208 | tf_op jit(solution)/shard_map/dot_general | solution.py:40
  117.4 1.9 %fusion.25 = f32[1024,384]{1,0:T(8,128)} fusion(bf16[1024,384]{1,0:T(8,128)(2,1)S(1)} %bitcast.190, bf16[3,3,3,384,384]{4,3,2,1,0:T(8,128)(2,1)S(1)} %bitcast.185), kind=kOutput, calls=%fused_computation.85 | convolution fusion | flops 301989888 | bytes 2654208 | tf_op jit(solution)/shard_map/dot_general | solution.py:40
  119.3 1.8 %fusion.23 = f32[1024,384]{1,0:T(8,128)} fusion(bf16[1024,384]{1,0:T(8,128)(2,1)S(1)} %bitcast.189, bf16[3,3,3,384,384]{4,3,2,1,0:T(8,128)(2,1)S(1)} %bitcast.185), kind=kOutput, calls=%fused_computation.83 | convolution fusion | flops 301989888 | bytes 2654208 | tf_op jit(solution)/shard_map/dot_general | solution.py:40
  121.0 1.8 %fusion.21 = f32[1024,384]{1,0:T(8,128)} fusion(bf16[1024,384]{1,0:T(8,128)(2,1)S(1)} %bitcast.188, bf16[3,3,3,384,384]{4,3,2,1,0:T(8,128)(2,1)S(1)} %bitcast.185), kind=kOutput, calls=%fused_computation.81 | convolution fusion | flops 301989888 | bytes 2654208 | tf_op jit(solution)/shard_map/dot_general | solution.py:40
  122.8 13.2 %add_add_fusion = f32[1024,384]{1,0:T(8,128)S(1)} fusion(f32[1024,384]{1,0:T(8,128)} %fusion.12, f32[1024,384]{1,0:T(8,128)S(1)} %fusion.14, f32[1024,384]{1,0:T(8,128)S(1)} %fusion.16, f32[1024,384]{1,0:T(8,128)} %fusion.3, f32[1024,384]{1,0:T(8,128)S(1)} %fusion.19, f32[1024,384]{1,0:T(8,128)} %fusion.21, f32[1024,384]{1,0:T(8,128)} %fusion.23, ...), kind=kOutput, calls=%fused_computation.30 | convolution fusion | flops 312606720 | bytes 43550208 | tf_op jit(solution)/shard_map/dot_general | solution.py:40
  136.3 2.1 %collective-permute-start.2 = (bf16[2,16,32,384]{3,2,1,0:T(8,128)(2,1)S(1)}, bf16[2,16,32,384]{3,2,1,0:T(8,128)(2,1)S(1)}, u32[]{:S(2)}, u32[]{:S(2)}) collective-permute-start(bf16[2,16,32,384]{3,2,1,0:T(8,128)(2,1)S(1)} %add_convert_fusion.2), channel_id=1, source_target_pairs={{0,1},{1,2},{2,3},{3,4},{4,5},{5,6},{6,7},{7,8},{8,9},{9,10},{10,1... | collective-permute-start | bytes 2359304 | tf_op jit(solution)/shard_map/ppermute | solution.py:15
  138.4 1.0 fusion.1
  139.4 11.3 %collective-permute-done.2 = bf16[2,16,32,384]{3,2,1,0:T(8,128)(2,1)S(1)} collective-permute-done((bf16[2,16,32,384]{3,2,1,0:T(8,128)(2,1)S(1)}, bf16[2,16,32,384]{3,2,1,0:T(8,128)(2,1)S(1)}, u32[]{:S(2)}, u32[]{:S(2)}) %collective-permute-start.2) | collective-permute-done | bytes 786464 | tf_op jit(solution)/shard_map/ppermute | solution.py:15
  150.8 1.0 fusion.5
  151.8 1.0 add_convert_fusion
  153.2 1.4 copy.68
  (158 shorter events, 26.8 us)
Async XLA Ops:
  0.0 58.4 %copy-start = (bf16[3,3,3,16,384]{4,3,2,1,0:T(8,128)(2,1)S(1)}, bf16[3,3,3,16,384]{4,3,2,1,0:T(8,128)(2,1)}, u32[]{:S(2)}) copy-start(bf16[3,3,3,16,384]{4,3,2,1,0:T(8,128)(2,1)} %param.9) | copy-start | bytes 995332
  12.2 8.6 %collective-permute-start = (bf16[2,16,32,16]{3,2,1,0:T(8,128)(2,1)S(1)}, bf16[2,16,32,16]{3,2,1,0:T(8,128)(2,1)S(1)}, u32[]{:S(2)}, u32[]{:S(2)}) collective-permute-start(bf16[2,16,32,16]{3,2,1,0:T(8,128)(2,1)S(1)} %reshape.157), channel_id=1, source_target_pairs={{0,1},{1,2},{2,3},{3,4},{4,5},{5,6},{6,7},{7,8},{8,9},{9,10},{10,1... | collective-permute-start | bytes 98312 | tf_op jit(solution)/shard_map/ppermute | solution.py:15
  26.0 14.0 %copy-start.27 = (bf16[2,16,32,16]{3,2,1,0:T(8,128)(2,1)S(1)}, bf16[2,16,32,16]{3,2,1,0:T(8,128)(2,1)}, u32[]{:S(2)}) copy-start(bf16[2,16,32,16]{3,2,1,0:T(8,128)(2,1)} %get-tuple-element.36) | copy-start | bytes 98308
  26.8 14.0 %copy-start.26 = (bf16[2,16,32,16]{3,2,1,0:T(8,128)(2,1)S(1)}, bf16[2,16,32,16]{3,2,1,0:T(8,128)(2,1)}, u32[]{:S(2)}) copy-start(bf16[2,16,32,16]{3,2,1,0:T(8,128)(2,1)} %get-tuple-element.37) | copy-start | bytes 98308
  27.5 13.4 %copy-start.25 = (bf16[2,16,32,16]{3,2,1,0:T(8,128)(2,1)S(1)}, bf16[2,16,32,16]{3,2,1,0:T(8,128)(2,1)}, u32[]{:S(2)}) copy-start(bf16[2,16,32,16]{3,2,1,0:T(8,128)(2,1)} %get-tuple-element.38) | copy-start | bytes 98308
  27.6 13.5 %copy-start.24 = (bf16[2,16,32,16]{3,2,1,0:T(8,128)(2,1)S(1)}, bf16[2,16,32,16]{3,2,1,0:T(8,128)(2,1)}, u32[]{:S(2)}) copy-start(bf16[2,16,32,16]{3,2,1,0:T(8,128)(2,1)} %get-tuple-element.39) | copy-start | bytes 98308
  28.3 13.0 %copy-start.23 = (bf16[2,16,32,16]{3,2,1,0:T(8,128)(2,1)S(1)}, bf16[2,16,32,16]{3,2,1,0:T(8,128)(2,1)}, u32[]{:S(2)}) copy-start(bf16[2,16,32,16]{3,2,1,0:T(8,128)(2,1)} %get-tuple-element.40) | copy-start | bytes 98308
  30.0 11.4 %copy-start.22 = (bf16[2,16,32,16]{3,2,1,0:T(8,128)(2,1)S(1)}, bf16[2,16,32,16]{3,2,1,0:T(8,128)(2,1)}, u32[]{:S(2)}) copy-start(bf16[2,16,32,16]{3,2,1,0:T(8,128)(2,1)} %get-tuple-element.41) | copy-start | bytes 98308
  31.7 9.8 %copy-start.21 = (bf16[2,16,32,16]{3,2,1,0:T(8,128)(2,1)S(1)}, bf16[2,16,32,16]{3,2,1,0:T(8,128)(2,1)}, u32[]{:S(2)}) copy-start(bf16[2,16,32,16]{3,2,1,0:T(8,128)(2,1)} %get-tuple-element.42) | copy-start | bytes 98308
  40.8 1.4 copy-start.39
  40.9 2.0 %copy-start.40 = (bf16[1024,16]{0,1:T(8,128)(2,1)S(1)}, bf16[1024,16]{0,1:T(8,128)(2,1)}, u32[]{:S(2)}) copy-start(bf16[1024,16]{0,1:T(8,128)(2,1)} %copy.71) | copy-start | bytes 98308
  40.9 2.6 %copy-start.38 = (bf16[1024,16]{0,1:T(8,128)(2,1)S(1)}, bf16[1024,16]{0,1:T(8,128)(2,1)}, u32[]{:S(2)}) copy-start(bf16[1024,16]{0,1:T(8,128)(2,1)} %copy.72) | copy-start | bytes 98308
  41.0 3.2 %copy-start.33 = (bf16[1024,16]{0,1:T(8,128)(2,1)S(1)}, bf16[1024,16]{0,1:T(8,128)(2,1)}, u32[]{:S(2)}) copy-start(bf16[1024,16]{0,1:T(8,128)(2,1)} %copy.73) | copy-start | bytes 98308
  41.0 3.8 %copy-start.37 = (bf16[1024,16]{0,1:T(8,128)(2,1)S(1)}, bf16[1024,16]{0,1:T(8,128)(2,1)}, u32[]{:S(2)}) copy-start(bf16[1024,16]{0,1:T(8,128)(2,1)} %copy.74) | copy-start | bytes 98308
  41.1 4.3 %copy-start.36 = (bf16[1024,16]{0,1:T(8,128)(2,1)S(1)}, bf16[1024,16]{0,1:T(8,128)(2,1)}, u32[]{:S(2)}) copy-start(bf16[1024,16]{0,1:T(8,128)(2,1)} %copy.75) | copy-start | bytes 98308
  41.1 4.9 %copy-start.35 = (bf16[1024,16]{0,1:T(8,128)(2,1)S(1)}, bf16[1024,16]{0,1:T(8,128)(2,1)}, u32[]{:S(2)}) copy-start(bf16[1024,16]{0,1:T(8,128)(2,1)} %copy.76) | copy-start | bytes 98308
  41.1 5.5 %copy-start.34 = (bf16[1024,16]{0,1:T(8,128)(2,1)S(1)}, bf16[1024,16]{0,1:T(8,128)(2,1)}, u32[]{:S(2)}) copy-start(bf16[1024,16]{0,1:T(8,128)(2,1)} %copy.77) | copy-start | bytes 98308
  41.2 8.5 %copy-start.32 = (bf16[1024,16]{0,1:T(8,128)(2,1)S(1)}, bf16[1024,16]{0,1:T(8,128)(2,1)}, u32[]{:S(2)}) copy-start(bf16[1024,16]{0,1:T(8,128)(2,1)} %copy.82) | copy-start | bytes 98308
  41.5 13.2 %copy-start.31 = (bf16[1024,16]{0,1:T(8,128)(2,1)S(1)}, bf16[1024,16]{0,1:T(8,128)(2,1)}, u32[]{:S(2)}) copy-start(bf16[1024,16]{0,1:T(8,128)(2,1)} %copy.90) | copy-start | bytes 98308
  41.5 14.4 %copy-start.29 = (bf16[1024,16]{0,1:T(8,128)(2,1)S(1)}, bf16[1024,16]{0,1:T(8,128)(2,1)}, u32[]{:S(2)}) copy-start(bf16[1024,16]{0,1:T(8,128)(2,1)} %copy.91) | copy-start | bytes 98308
  41.6 14.9 %copy-start.28 = (bf16[1024,16]{0,1:T(8,128)(2,1)S(1)}, bf16[1024,16]{0,1:T(8,128)(2,1)}, u32[]{:S(2)}) copy-start(bf16[1024,16]{0,1:T(8,128)(2,1)} %copy.92) | copy-start | bytes 98308
  41.6 16.1 %copy-start.30 = (bf16[1024,16]{0,1:T(8,128)(2,1)S(1)}, bf16[1024,16]{0,1:T(8,128)(2,1)}, u32[]{:S(2)}) copy-start(bf16[1024,16]{0,1:T(8,128)(2,1)} %copy.94) | copy-start | bytes 98308
  41.6 16.7 %copy-start.44 = (f32[384]{0:T(512)S(1)}, f32[384]{0:T(512)}, u32[]{:S(2)}) copy-start(f32[384]{0:T(512)} %param.10) | copy-start | bytes 4612
  58.4 2.1 %copy-start.43 = (f32[384]{0:T(512)S(1)}, f32[384]{0:T(512)}, u32[]{:S(2)}) copy-start(f32[384]{0:T(512)} %param.11) | copy-start | bytes 4612
  61.0 14.2 %collective-permute-start.1 = (bf16[2,16,32,384]{3,2,1,0:T(8,128)(2,1)S(1)}, bf16[2,16,32,384]{3,2,1,0:T(8,128)(2,1)S(1)}, u32[]{:S(2)}, u32[]{:S(2)}) collective-permute-start(bf16[2,16,32,384]{3,2,1,0:T(8,128)(2,1)S(1)} %multiply_convert_fusion.1), channel_id=1, source_target_pairs={{0,1},{1,2},{2,3},{3,4},{4,5},{5,6},{6,7},{7,8},{8,9},{9,10},{10,1... | collective-permute-start | bytes 2359304 | tf_op jit(solution)/shard_map/ppermute | solution.py:15
  75.4 8.5 %slice-start = ((s8[7962624]{0:T(1024)(128)(4,1)}), s8[4194304]{0:T(1024)(128)(4,1)S(1)}, s32[]{:S(2)}) async-start(s8[7962624]{0:T(1024)(128)(4,1)} %bitcast.184), calls=%async_computation.1 | async-start | bytes 8388608
  77.5 6.3 %slice-start.1 = ((s8[7962624]{0:T(1024)(128)(4,1)}), s8[3768320]{0:T(1024)(128)(4,1)S(1)}, s32[]{:S(2)}) async-start(s8[7962624]{0:T(1024)(128)(4,1)} %bitcast.184), calls=%async_computation.2 | async-start | bytes 7536640
  87.1 1.2 copy-start.18
  88.2 1.8 %copy-start.17 = (bf16[2,16,32,384]{3,2,1,0:T(8,128)(2,1)S(1)}, bf16[2,16,32,384]{3,2,1,0:T(8,128)(2,1)}, u32[]{:S(2)}) copy-start(bf16[2,16,32,384]{3,2,1,0:T(8,128)(2,1)} %get-tuple-element.6) | copy-start | bytes 2359300
  90.0 1.8 %copy-start.16 = (bf16[2,16,32,384]{3,2,1,0:T(8,128)(2,1)S(1)}, bf16[2,16,32,384]{3,2,1,0:T(8,128)(2,1)}, u32[]{:S(2)}) copy-start(bf16[2,16,32,384]{3,2,1,0:T(8,128)(2,1)} %get-tuple-element.7) | copy-start | bytes 2359300
  91.8 1.8 %copy-start.15 = (bf16[2,16,32,384]{3,2,1,0:T(8,128)(2,1)S(1)}, bf16[2,16,32,384]{3,2,1,0:T(8,128)(2,1)}, u32[]{:S(2)}) copy-start(bf16[2,16,32,384]{3,2,1,0:T(8,128)(2,1)} %get-tuple-element.8) | copy-start | bytes 2359300
  93.6 1.8 %copy-start.14 = (bf16[2,16,32,384]{3,2,1,0:T(8,128)(2,1)S(1)}, bf16[2,16,32,384]{3,2,1,0:T(8,128)(2,1)}, u32[]{:S(2)}) copy-start(bf16[2,16,32,384]{3,2,1,0:T(8,128)(2,1)} %get-tuple-element.9) | copy-start | bytes 2359300
  95.4 1.8 %copy-start.13 = (bf16[2,16,32,384]{3,2,1,0:T(8,128)(2,1)S(1)}, bf16[2,16,32,384]{3,2,1,0:T(8,128)(2,1)}, u32[]{:S(2)}) copy-start(bf16[2,16,32,384]{3,2,1,0:T(8,128)(2,1)} %get-tuple-element.10) | copy-start | bytes 2359300
  97.2 1.8 %copy-start.12 = (bf16[2,16,32,384]{3,2,1,0:T(8,128)(2,1)S(1)}, bf16[2,16,32,384]{3,2,1,0:T(8,128)(2,1)}, u32[]{:S(2)}) copy-start(bf16[2,16,32,384]{3,2,1,0:T(8,128)(2,1)} %get-tuple-element.11) | copy-start | bytes 2359300
  99.1 1.8 %copy-start.11 = (bf16[2,16,32,384]{3,2,1,0:T(8,128)(2,1)S(1)}, bf16[2,16,32,384]{3,2,1,0:T(8,128)(2,1)}, u32[]{:S(2)}) copy-start(bf16[2,16,32,384]{3,2,1,0:T(8,128)(2,1)} %get-tuple-element.12) | copy-start | bytes 2359300
  100.8 1.9 %copy-start.10 = (bf16[2,16,32,384]{3,2,1,0:T(8,128)(2,1)S(1)}, bf16[2,16,32,384]{3,2,1,0:T(8,128)(2,1)}, u32[]{:S(2)}) copy-start(bf16[2,16,32,384]{3,2,1,0:T(8,128)(2,1)} %get-tuple-element.13) | copy-start | bytes 2359300
  102.7 1.8 %copy-start.9 = (bf16[2,16,32,384]{3,2,1,0:T(8,128)(2,1)S(1)}, bf16[2,16,32,384]{3,2,1,0:T(8,128)(2,1)}, u32[]{:S(2)}) copy-start(bf16[2,16,32,384]{3,2,1,0:T(8,128)(2,1)} %get-tuple-element.14) | copy-start | bytes 2359300
  104.5 1.8 %copy-start.8 = (bf16[2,16,32,384]{3,2,1,0:T(8,128)(2,1)S(1)}, bf16[2,16,32,384]{3,2,1,0:T(8,128)(2,1)}, u32[]{:S(2)}) copy-start(bf16[2,16,32,384]{3,2,1,0:T(8,128)(2,1)} %get-tuple-element.15) | copy-start | bytes 2359300
  106.3 1.8 %copy-start.7 = (bf16[2,16,32,384]{3,2,1,0:T(8,128)(2,1)S(1)}, bf16[2,16,32,384]{3,2,1,0:T(8,128)(2,1)}, u32[]{:S(2)}) copy-start(bf16[2,16,32,384]{3,2,1,0:T(8,128)(2,1)} %get-tuple-element.16) | copy-start | bytes 2359300
  108.1 1.8 %copy-start.6 = (bf16[2,16,32,384]{3,2,1,0:T(8,128)(2,1)S(1)}, bf16[2,16,32,384]{3,2,1,0:T(8,128)(2,1)}, u32[]{:S(2)}) copy-start(bf16[2,16,32,384]{3,2,1,0:T(8,128)(2,1)} %get-tuple-element.17) | copy-start | bytes 2359300
  109.9 1.8 %copy-start.5 = (bf16[2,16,32,384]{3,2,1,0:T(8,128)(2,1)S(1)}, bf16[2,16,32,384]{3,2,1,0:T(8,128)(2,1)}, u32[]{:S(2)}) copy-start(bf16[2,16,32,384]{3,2,1,0:T(8,128)(2,1)} %get-tuple-element.18) | copy-start | bytes 2359300
  111.6 1.8 %copy-start.4 = (bf16[2,16,32,384]{3,2,1,0:T(8,128)(2,1)S(1)}, bf16[2,16,32,384]{3,2,1,0:T(8,128)(2,1)}, u32[]{:S(2)}) copy-start(bf16[2,16,32,384]{3,2,1,0:T(8,128)(2,1)} %get-tuple-element.19) | copy-start | bytes 2359300
  113.5 2.1 %copy-start.3 = (bf16[2,16,32,384]{3,2,1,0:T(8,128)(2,1)S(1)}, bf16[2,16,32,384]{3,2,1,0:T(8,128)(2,1)}, u32[]{:S(2)}) copy-start(bf16[2,16,32,384]{3,2,1,0:T(8,128)(2,1)} %get-tuple-element.20) | copy-start | bytes 2359300
  115.5 1.9 %copy-start.2 = (bf16[2,16,32,384]{3,2,1,0:T(8,128)(2,1)S(1)}, bf16[2,16,32,384]{3,2,1,0:T(8,128)(2,1)}, u32[]{:S(2)}) copy-start(bf16[2,16,32,384]{3,2,1,0:T(8,128)(2,1)} %get-tuple-element.21) | copy-start | bytes 2359300
  121.0 1.8 %copy-start.42 = (f32[384]{0:T(512)S(1)}, f32[384]{0:T(512)}, u32[]{:S(2)}) copy-start(f32[384]{0:T(512)} %param.13) | copy-start | bytes 4612
  136.0 2.4 %copy-start.20 = (bf16[3,384,768]{2,1,0:T(8,128)(2,1)S(1)}, bf16[3,384,768]{2,1,0:T(8,128)(2,1)}, u32[]{:S(2)}) copy-start(bf16[3,384,768]{2,1,0:T(8,128)(2,1)} %param.14) | copy-start | bytes 5308420
  136.3 14.3 %collective-permute-start.2 = (bf16[2,16,32,384]{3,2,1,0:T(8,128)(2,1)S(1)}, bf16[2,16,32,384]{3,2,1,0:T(8,128)(2,1)S(1)}, u32[]{:S(2)}, u32[]{:S(2)}) collective-permute-start(bf16[2,16,32,384]{3,2,1,0:T(8,128)(2,1)S(1)} %add_convert_fusion.2), channel_id=1, source_target_pairs={{0,1},{1,2},{2,3},{3,4},{4,5},{5,6},{6,7},{7,8},{8,9},{9,10},{10,1... | collective-permute-start | bytes 2359304 | tf_op jit(solution)/shard_map/ppermute | solution.py:15
  153.2 1.4 copy-start.1
  (2 other events, 2.1 us)
where the time goes:
time: 155 us
  matrix products  59.3 us (38%)
  local copies, waits for them, and re-layouts  49.7 us (32%)
  waiting for transfers between devices  26.8 us (17%)
  blocking collectives  11.1 us (7%)
  starting transfers between devices  6 us (4%)
    dot_general x30, matrix products, conv_valid(): jnp.dot(window.reshape(-1, inner), kernel, preferred_element_type=jnp.flo...  57.3 us
    ppermute x3, waiting for transfers between devices, passed_along(): return lax.ppermute(block, axis, route)  26.8 us
    concatenate x29, local copies, waits for them, and re-layouts, conv_input(): jnp.concatenate(windows, axis=-1).reshape(frames * rows * cols, 27 * inner)  18.7 us
    unnamed x121, local copies, waits for them, and re-layouts  16.8 us
    all_to_all x1, blocking collectives, per_device(): lax.all_to_all(latent, 'tm', split_axis=0, concat_axis=1, tiled=True)  11.1 us
    slice x2, local copies, waits for them, and re-layouts, conv_valid(): padded[step_t:step_t + frames, step_h:step_h + rows, step_w:step_w + cols...  8.35 us
    ppermute x3, starting transfers between devices, passed_along(): return lax.ppermute(block, axis, route)  6 us
  transfers between devices with their start and end apart: 3, of which 3 were waited for; matrix products, arithmetic and copies ran while one was open for 3% of the time, Pallas kernels for 0%

commit v1 on v0

v1 whole, which is shorter than its diff:
```python
import functools

import jax
import jax.numpy as jnp
from jax import lax
from jax.experimental import pallas as pl
from jax.experimental.pallas import tpu as pltpu
from jax.sharding import PartitionSpec as P

ZC = 16
C = 384
H = 16
W = 32
F = 2
KT = 64
ROW = W * ZC
WIDE = ROW + 128
MESH = pl.DeviceIdType.MESH
CHUNK = 16


def kernel(
    n, latent_ref, w_in_ref, b_in_ref, gain_ref, w_mid_ref, b_mid_ref, w_time_ref, b_time_ref,
    out_ref,
    padded, sent, got, spread, shifted, win, wmid, wtime, act3, hid, turn, own, halo,
    lat_send, lat_recv, halo_send, halo_recv, win_sem, wmid_sem, wtime_sem,
):
    me = lax.axis_index("tm")
    block = latent_ref.shape[1]
    frames = latent_ref.shape[0]
    per_row = ROW // block

    for t in range(9):
        pltpu.make_async_copy(w_in_ref.at[t], win.at[pl.ds(t * KT, 48)], win_sem.at[t]).start()
    for dt in range(3):
        for di in range(3):
            for dj in range(3):
                pltpu.make_async_copy(
                    w_mid_ref.at[dt, di, dj],
                    wmid.at[dt, pl.ds(dj * 3 * C + di * C, C)],
                    wmid_sem.at[dt * 9 + di * 3 + dj],
                ).start()
    pltpu.make_async_copy(w_time_ref, wtime, wtime_sem).start()

    barrier = pltpu.get_barrier_semaphore()

    def greet(o, carry):
        pl.semaphore_signal(
            barrier, inc=1, device_id={"tm": lax.rem(me + o, n)}, device_id_type=MESH
        )
        return carry

    lax.fori_loop(1, n, greet, 0)

    padded[pl.ds(0, 8), :] = jnp.zeros((8, block), jnp.float32)
    padded[pl.ds(frames, 16), :] = jnp.zeros((16, block), jnp.float32)
    padded[pl.ds(4, frames), :] = latent_ref[...].astype(jnp.float32)
    for d in range(n):
        sent[d] = padded[pl.ds(F * d, 8), :].astype(jnp.bfloat16)

    for t in range(9):
        win[pl.ds(t * KT + 48, 16), :] = jnp.zeros((16, C), jnp.bfloat16)
    win[pl.ds(9 * KT, KT), :] = jnp.zeros((KT, C), jnp.bfloat16)
    act3[0] = jnp.zeros(act3.shape[1:], jnp.bfloat16)
    act3[W + 1] = jnp.zeros(act3.shape[1:], jnp.bfloat16)

    pl.semaphore_wait(barrier, n - 1)

    def lat_copy(o):
        d = lax.rem(me + o, n)
        return pltpu.make_async_remote_copy(
            src_ref=sent.at[d], dst_ref=got.at[me], send_sem=lat_send.at[d],
            recv_sem=lat_recv.at[me], device_id={"tm": d}, device_id_type=MESH,
        )

    def send(o, carry):
        lat_copy(o).start()
        return carry

    lax.fori_loop(1, n, send, 0)
    got[me] = sent[me]

    def receive(o, carry):
        j = lax.rem(me + o, n)
        pltpu.make_async_remote_copy(
            src_ref=sent.at[j], dst_ref=got.at[j], send_sem=lat_send.at[j],
            recv_sem=lat_recv.at[j], device_id={"tm": j}, device_id_type=MESH,
        ).wait_recv()
        return carry

    lax.fori_loop(1, n, receive, 0)

    flat = got[...].astype(jnp.float32).reshape(n * 8, block)
    for c in range(block // 128):
        spread[c] = flat[:, c * 128 : (c + 1) * 128]
    picked = []
    for s in range(F + 4):
        parts = [
            spread[c, pl.ds(b * 8 + s, H, stride=8 * per_row), :]
            for b in range(per_row)
            for c in range(block // 128)
        ]
        parts.append(jnp.zeros((H, 128), jnp.float32))
        picked.append(jnp.concatenate(parts, axis=1))
    lat = jnp.concatenate(picked, axis=0)
    total = (F + 4) * H
    row_of = lax.broadcasted_iota(jnp.int32, (total, WIDE), 0) & (H - 1)
    for di in range(3):
        if di == 0:
            moved = jnp.where(row_of == 0, 0.0, pltpu.roll(lat, 1, 0))
        elif di == 2:
            moved = jnp.where(row_of == H - 1, 0.0, pltpu.roll(lat, total - 1, 0))
        else:
            moved = lat
        shifted[0, di] = moved
        shifted[1, di] = pltpu.roll(moved, KT, 1)

    for t in range(9):
        pltpu.make_async_copy(w_in_ref.at[t], win.at[pl.ds(t * KT, 48)], win_sem.at[t]).wait()

    wide = (F + 2) * H
    rows = 4 * wide
    first = jnp.where(me > 0, 0, 2)

    def columns(k, carry):
        lane = lax.broadcasted_iota(jnp.int32, (wide, WIDE), 1)
        even = ((lane - ZC * (k - 1)) & 127) < KT
        turnby = lax.rem(WIDE + ZC - ZC * k, WIDE)
        pieces = []
        for p in range(5):
            dt, di = divmod(2 * p, 3)
            both = shifted[0, di, pl.ds(dt * H, wide), :]
            if p < 4:
                dt, di = divmod(2 * p + 1, 3)
                both = jnp.where(even, both, shifted[1, di, pl.ds(dt * H, wide), :])
            pieces.append(pltpu.roll(both, turnby, 1)[:, :ROW].astype(jnp.bfloat16))
        left = jnp.concatenate(
            [
                jnp.concatenate([piece[:, g * 128 : (g + 1) * 128] for piece in pieces], axis=1)
                for g in range(4)
            ],
            axis=0,
        )
        h0 = jnp.dot(left, win[...], preferred_element_type=jnp.float32) + b_in_ref[...]
        h0 = h0.astype(jnp.bfloat16)
        values = h0.astype(jnp.float32)
        scale = lax.rsqrt(jnp.mean(values * values, axis=-1, keepdims=True) + 1e-06)
        v = values * scale * gain_ref[...]
        act = v / (1.0 + jnp.exp(-v))
        row = lax.broadcasted_iota(jnp.int32, (rows, C), 0)
        act = jnp.where(((row >> 4) & 3) >= first, act, 0.0)
        above = jnp.where((row & (H - 1)) == 0, 0.0, pltpu.roll(act, 1, 0))
        below = jnp.where((row & (H - 1)) == H - 1, 0.0, pltpu.roll(act, rows - 1, 0))
        trio = [x.astype(jnp.bfloat16) for x in (above, act, below)]
        for g in range(4):
            for di in range(3):
                for a in range(F + 2):
                    act3[g * 8 + k + 1, a, :, pl.ds(di * C, C)] = trio[di][
                        g * wide + a * H : g * wide + (a + 1) * H
                    ]
            for a in range(F):
                hid[g * 8 + k, a] = h0[g * wide + (a + 2) * H : g * wide + (a + 3) * H]
        return carry

    lax.fori_loop(0, 8, columns, 0)

    for dt in range(3):
        for di in range(3):
            for dj in range(3):
                pltpu.make_async_copy(
                    w_mid_ref.at[dt, di, dj],
                    wmid.at[dt, pl.ds(dj * 3 * C + di * C, C)],
                    wmid_sem.at[dt * 9 + di * 3 + dj],
                ).wait()

    after = lax.rem(me + 1, n)

    def halo_copy(m):
        f = m // (W // CHUNK)
        w0 = pl.multiple_of(lax.rem(m, W // CHUNK) * CHUNK, CHUNK)
        return pltpu.make_async_remote_copy(
            src_ref=own.at[f, :, pl.ds(w0, CHUNK)], dst_ref=halo.at[f, :, pl.ds(w0, CHUNK)],
            send_sem=halo_send.at[m], recv_sem=halo_recv.at[m],
            device_id={"tm": after}, device_id_type=MESH,
        )

    def residual(m, carry):
        f = m // (W // CHUNK)
        w0 = pl.multiple_of(lax.rem(m, W // CHUNK) * CHUNK, CHUNK)
        acc = hid[pl.ds(w0, CHUNK), f].astype(jnp.float32).reshape(CHUNK * H, C) + b_mid_ref[...]
        for dt in range(3):
            left = jnp.concatenate(
                [
                    act3[pl.ds(w0 + dj, CHUNK), f + dt].reshape(CHUNK * H, 3 * C)
                    for dj in range(3)
                ],
                axis=1,
            )
            acc = acc + jnp.dot(left, wmid[dt], preferred_element_type=jnp.float32)
        for c in range(C // 128):
            turn[c] = acc[:, c * 128 : (c + 1) * 128]
        for i in range(H):
            line = [turn[c, pl.ds(i, CHUNK, stride=H), :] for c in range(C // 128)]
            own[f, i, pl.ds(w0, CHUNK)] = jnp.concatenate(line, axis=1).astype(jnp.bfloat16)

        @pl.when(me < n - 1)
        def _():
            halo_copy(m).start()

        return carry

    chunks = F * (W // CHUNK)
    lax.fori_loop(0, chunks, residual, 0)

    pltpu.make_async_copy(w_time_ref, wtime, wtime_sem).wait()

    @pl.when(me > 0)
    def _():
        for m in range(chunks):
            halo_copy(m).wait_recv()

    @pl.when(me == 0)
    def _():
        halo[...] = jnp.zeros(halo.shape, jnp.bfloat16)

    def upsample(q, carry):
        i0 = q * 4
        blocks = [
            (halo if f < 2 else own)[f % 2, pl.ds(i0, 4)].reshape(4 * W, C) for f in range(4)
        ]
        for f in range(F):
            left = jnp.concatenate(blocks[f : f + 3], axis=1)
            up = jnp.dot(left, wtime[...], preferred_element_type=jnp.float32) + b_time_ref[...]
            up = up.astype(jnp.bfloat16)
            for s in range(2):
                out_ref[2 * f + s, pl.ds(i0, 4)] = up[:, s * C : (s + 1) * C].reshape(4, W, C)
        return carry

    lax.fori_loop(0, H // 4, upsample, 0)

    def sent_all(o, carry):
        lat_copy(o).wait_send()
        return carry

    lax.fori_loop(1, n, sent_all, 0)

    @pl.when(me < n - 1)
    def _():
        for m in range(chunks):
            halo_copy(m).wait_send()


def per_device(n, latent, w_in, b_in, gain, w_mid, b_mid, w_time, b_time):
    frames, block = latent.shape
    assert frames == F * n
    bf16, f32 = jnp.bfloat16, jnp.float32
    vmem = pl.BlockSpec(memory_space=pltpu.VMEM)
    hbm = pl.BlockSpec(memory_space=pl.ANY)
    chunks = F * (W // CHUNK)
    dma = pltpu.SemaphoreType.DMA
    return pl.pallas_call(
        functools.partial(kernel, n),
        out_shape=jax.ShapeDtypeStruct((2 * F, H, W, C), bf16),
        in_specs=[vmem, hbm, vmem, vmem, hbm, vmem, hbm, vmem],
        out_specs=vmem,
        scratch_shapes=[
            pltpu.VMEM((frames + 16, block), f32),
            pltpu.VMEM((n, 8, block), bf16),
            pltpu.VMEM((n, 8, block), bf16),
            pltpu.VMEM((block // 128, n * 8, 128), f32),
            pltpu.VMEM((2, 3, (F + 4) * H, WIDE), f32),
            pltpu.VMEM((10 * KT, C), bf16),
            pltpu.VMEM((3, 9 * C, C), bf16),
            pltpu.VMEM((3 * C, 2 * C), bf16),
            pltpu.VMEM((W + 2, F + 2, H, 3 * C), bf16),
            pltpu.VMEM((W, F, H, C), bf16),
            pltpu.VMEM((C // 128, CHUNK * H, 128), f32),
            pltpu.VMEM((F, H, W, C), bf16),
            pltpu.VMEM((F, H, W, C), bf16),
            dma((n,)), dma((n,)), dma((chunks,)), dma((chunks,)), dma((9,)), dma((27,)), dma(()),
        ],
        compiler_params=pltpu.CompilerParams(
            collective_id=0, has_side_effects=True, vmem_limit_bytes=48 * 1024 * 1024
        ),
        name="decoder_window",
    )(
        latent,
        w_in.reshape(9, 3 * ZC, C),
        b_in.reshape(1, C),
        gain.reshape(1, C),
        w_mid,
        b_mid.reshape(1, C),
        w_time.reshape(3 * C, 2 * C),
        b_time.reshape(1, 2 * C),
    )


def solution(mesh):
    n = mesh.shape["tm"]
    return jax.shard_map(
        functools.partial(per_device, n),
        mesh=mesh,
        in_specs=(P("groups", "tm"), P(), P(), P(), P(), P(), P(), P()),
        out_specs=P(("groups", "tm"), None, None, None),
        check_vma=False,
    )
```

time: 155 us -> 43.5 us (0.28)
  matrix products: 59.3 us -> 0 us
  local copies, waits for them, and re-layouts: 49.7 us -> 7.09 us
  Pallas kernels: 0 us -> 36 us
  waiting for transfers between devices: 26.8 us -> 0 us
  blocking collectives: 11.1 us -> 0 us
  starting transfers between devices: 6 us -> 0 us
    dot_general x31 -> x0, matrix products: 59.3 us -> none  [the longest x30 57.3 us: conv_valid(): jnp.dot(window.reshape(-1, inner), kernel, preferred_element_type=jnp.flo...]
    pallas_call x0 -> x1, Pallas kernels: none -> 36 us  [per_device(): pl.pallas_call(functools.partial(kernel, n), out_shape=jax.ShapeDtypeStru...]
    ppermute x3 -> x0, waiting for transfers between devices: 26.8 us -> none  [passed_along(): return lax.ppermute(block, axis, route)]
    concatenate x30 -> x0, local copies, waits for them, and re-layouts: 18.7 us -> none  [the longest x29 18.7 us: conv_input(): jnp.concatenate(windows, axis=-1).reshape(frames * rows * cols, 27 * inner)]
    unnamed x121 -> x7, local copies, waits for them, and re-layouts: 16.8 us -> 4.35 us
    slice x4 -> x0, local copies, waits for them, and re-layouts: 11.2 us -> none  [the longest x2 8.35 us: conv_valid(): padded[step_t:step_t + frames, step_h:step_h + rows, step_w:step_w + cols...]
    all_to_all x1 -> x0, blocking collectives: 11.1 us -> none  [per_device(): lax.all_to_all(latent, 'tm', split_axis=0, concat_axis=1, tiled=True)]
    ppermute x3 -> x0, starting transfers between devices: 6 us -> none  [passed_along(): return lax.ppermute(block, axis, route)]
  transfers between devices with their start and end apart: 3 -> 0, of which waited for: 3 -> 0; matrix products, arithmetic and copies ran while one was open for 3% -> 0% of each run, Pallas kernels for 0% -> 0%
where the time goes in v1:
time: 43.5 us; the launch traced here: 43.1 us
  Pallas kernels  36 us (83%)
  local copies, waits for them, and re-layouts  7.09 us (16%)
    pallas_call x1, Pallas kernels, per_device(): pl.pallas_call(functools.partial(kernel, n), out_shape=jax.ShapeDtypeStru...  36 us
    unnamed x7, local copies, waits for them, and re-layouts  4.35 us

profile of v1, /device:TPU:8, one launch (start us, length us, event | category | flops | bytes accessed | tf_op | source)
XLA Modules:
  0.0 43.1 jit_solution(5715481269744947473)
XLA Ops:
  0.0 0.7 %reshape.19.b_in_ref = f32[1,384]{1,0:T(1,128)S(1)} reshape(f32[384]{0:T(512)} %param.10) | data formatting | bytes 3072 | tf_op jit(solution)/shard_map/reshape | solution.py:289
  0.7 0.7 %reshape.20.gain_ref = f32[1,384]{1,0:T(1,128)S(1)} reshape(f32[384]{0:T(512)} %param.11) | data formatting | bytes 3072 | tf_op jit(solution)/shard_map/reshape | solution.py:290
  1.4 0.7 %reshape.21.b_mid_ref = f32[1,384]{1,0:T(1,128)S(1)} reshape(f32[384]{0:T(512)} %param.13) | data formatting | bytes 3072 | tf_op jit(solution)/shard_map/reshape | solution.py:292
  2.0 0.7 %reshape.23.b_time_ref = f32[1,768]{1,0:T(1,128)S(1)} reshape(f32[768]{0:T(1024)} %param.15) | data formatting | bytes 6144 | tf_op jit(solution)/shard_map/reshape | solution.py:294
  2.7 0.0 copy-start
  2.7 1.5 %copy-done = bf16[3,384,768]{2,1,0:T(8,128)(2,1)S(1)} copy-done((bf16[3,384,768]{2,1,0:T(8,128)(2,1)S(1)}, bf16[3,384,768]{2,1,0:T(8,128)(2,1)}, u32[]{:S(2)}) %copy-start) | copy-done | bytes 1769496
  4.2 0.0 copy-start.1
  4.2 1.0 %copy-done.1 = bf16[3,3,3,16,384]{4,3,2,1,0:T(8,128)(2,1)S(1)} copy-done((bf16[3,3,3,16,384]{4,3,2,1,0:T(8,128)(2,1)S(1)}, bf16[3,3,3,16,384]{4,3,2,1,0:T(8,128)(2,1)}, u32[]{:S(2)}) %copy-start.1) | copy-done | bytes 331800
  5.2 0.0 copy-start.2
  5.2 0.8 %copy-done.2 = bf16[32,512]{1,0:T(8,128)(2,1)S(1)} copy-done((bf16[32,512]{1,0:T(8,128)(2,1)S(1)}, bf16[32,512]{1,0:T(8,128)(2,1)}, u32[]{:S(2)}) %copy-start.2) | copy-done | bytes 32792
  5.9 36.0 %decoder_window.1 = bf16[4,16,32,384]{3,2,1,0:T(8,128)(2,1)S(1)} custom-call(bf16[32,512]{1,0:T(8,128)(2,1)S(1)} %copy-done.2, bf16[9,48,384]{2,1,0:T(8,128)(2,1)S(1)} %bitcast.3, f32[1,384]{1,0:T(1,128)S(1)} %reshape.19.b_in_ref, f32[1,384]{1,0:T(1,128)S(1)} %reshape.20.gain_ref, bf16[3,3,3,384,384]{4,3,2,1,0:T(8,128)(2,1)} %w_mid_ref.1, ...), custom_call_target="tpu_custom_call" | custom-call | tf_op jit(solution)/shard_map/decoder_window/pallas_call | solution.py:261
  42.0 1.1 %copy.10 = bf16[4,16,32,384]{3,2,1,0:T(8,128)(2,1)} copy(bf16[4,16,32,384]{3,2,1,0:T(8,128)(2,1)S(1)} %decoder_window.1) | data formatting | bytes 3145728
Async XLA Ops:
  2.7 1.5 %copy-start = (bf16[3,384,768]{2,1,0:T(8,128)(2,1)S(1)}, bf16[3,384,768]{2,1,0:T(8,128)(2,1)}, u32[]{:S(2)}) copy-start(bf16[3,384,768]{2,1,0:T(8,128)(2,1)} %param.14) | copy-start | bytes 5308420
  4.2 1.0 %copy-start.1 = (bf16[3,3,3,16,384]{4,3,2,1,0:T(8,128)(2,1)S(1)}, bf16[3,3,3,16,384]{4,3,2,1,0:T(8,128)(2,1)}, u32[]{:S(2)}) copy-start(bf16[3,3,3,16,384]{4,3,2,1,0:T(8,128)(2,1)} %param.9) | copy-start | bytes 995332
  5.2 0.8 %copy-start.2 = (bf16[32,512]{1,0:T(8,128)(2,1)S(1)}, bf16[32,512]{1,0:T(8,128)(2,1)}, u32[]{:S(2)}) copy-start(bf16[32,512]{1,0:T(8,128)(2,1)} %latent_ref.1) | copy-start | bytes 98308

commit v2 on v1

--- a/solution.py
+++ b/solution.py
@@ -22,24 +22,33 @@
 def kernel(
     n, latent_ref, w_in_ref, b_in_ref, gain_ref, w_mid_ref, b_mid_ref, w_time_ref, b_time_ref,
     out_ref,
-    padded, sent, got, spread, shifted, win, wmid, wtime, act3, hid, turn, own, halo,
-    lat_send, lat_recv, halo_send, halo_recv, win_sem, wmid_sem, wtime_sem,
+    b_in, gain, b_mid, b_time, mine, padded, sent, got, spread, shifted, win, wmid, wtime, act_ref, hid, turn, own, halo,
+    lat_send, lat_recv, halo_send, halo_recv, win_sem, wmid_sem, wtime_sem, mine_sem, vec_sem,
 ):
     me = lax.axis_index("tm")
     block = latent_ref.shape[1]
     frames = latent_ref.shape[0]
     per_row = ROW // block
 
+    mine_copy = pltpu.make_async_copy(latent_ref, mine, mine_sem)
+    mine_copy.start()
+    vectors = ((b_in_ref, b_in), (gain_ref, gain), (b_mid_ref, b_mid), (b_time_ref, b_time))
+    vec_copies = [
+        pltpu.make_async_copy(src, dst, vec_sem.at[v]) for v, (src, dst) in enumerate(vectors)
+    ]
+    for copy in vec_copies:
+        copy.start()
     for t in range(9):
         pltpu.make_async_copy(w_in_ref.at[t], win.at[pl.ds(t * KT, 48)], win_sem.at[t]).start()
-    for dt in range(3):
-        for di in range(3):
-            for dj in range(3):
-                pltpu.make_async_copy(
-                    w_mid_ref.at[dt, di, dj],
-                    wmid.at[dt, pl.ds(dj * 3 * C + di * C, C)],
-                    wmid_sem.at[dt * 9 + di * 3 + dj],
-                ).start()
+    mid_copies = [
+        pltpu.make_async_copy(
+            w_mid_ref.at[dt, di], wmid.at[dt, :, :, pl.ds(di * C, C)], wmid_sem.at[dt * 3 + di]
+        )
+        for dt in range(3)
+        for di in range(3)
+    ]
+    for copy in mid_copies:
+        copy.start()
     pltpu.make_async_copy(w_time_ref, wtime, wtime_sem).start()
 
     barrier = pltpu.get_barrier_semaphore()
@@ -54,15 +63,16 @@
 
     padded[pl.ds(0, 8), :] = jnp.zeros((8, block), jnp.float32)
     padded[pl.ds(frames, 16), :] = jnp.zeros((16, block), jnp.float32)
-    padded[pl.ds(4, frames), :] = latent_ref[...].astype(jnp.float32)
+    mine_copy.wait()
+    padded[pl.ds(4, frames), :] = mine[...].astype(jnp.float32)
     for d in range(n):
         sent[d] = padded[pl.ds(F * d, 8), :].astype(jnp.bfloat16)
 
     for t in range(9):
         win[pl.ds(t * KT + 48, 16), :] = jnp.zeros((16, C), jnp.bfloat16)
     win[pl.ds(9 * KT, KT), :] = jnp.zeros((KT, C), jnp.bfloat16)
-    act3[0] = jnp.zeros(act3.shape[1:], jnp.bfloat16)
-    act3[W + 1] = jnp.zeros(act3.shape[1:], jnp.bfloat16)
+    act_ref[0] = jnp.zeros(act_ref.shape[1:], jnp.bfloat16)
+    act_ref[W + 1] = jnp.zeros(act_ref.shape[1:], jnp.bfloat16)
 
     pl.semaphore_wait(barrier, n - 1)
 
@@ -118,6 +128,9 @@
     for t in range(9):
         pltpu.make_async_copy(w_in_ref.at[t], win.at[pl.ds(t * KT, 48)], win_sem.at[t]).wait()
 
+    for copy in vec_copies:
+        copy.wait()
+
     wide = (F + 2) * H
     rows = 4 * wide
     first = jnp.where(me > 0, 0, 2)
@@ -141,37 +154,28 @@
             ],
             axis=0,
         )
-        h0 = jnp.dot(left, win[...], preferred_element_type=jnp.float32) + b_in_ref[...]
+        h0 = jnp.dot(left, win[...], preferred_element_type=jnp.float32) + b_in[...][None, :]
         h0 = h0.astype(jnp.bfloat16)
         values = h0.astype(jnp.float32)
         scale = lax.rsqrt(jnp.mean(values * values, axis=-1, keepdims=True) + 1e-06)
-        v = values * scale * gain_ref[...]
-        act = v / (1.0 + jnp.exp(-v))
+        v = values * scale * gain[...][None, :]
+        half = 0.5 * v
+        act = half + half * jnp.tanh(half)
         row = lax.broadcasted_iota(jnp.int32, (rows, C), 0)
         act = jnp.where(((row >> 4) & 3) >= first, act, 0.0)
-        above = jnp.where((row & (H - 1)) == 0, 0.0, pltpu.roll(act, 1, 0))
-        below = jnp.where((row & (H - 1)) == H - 1, 0.0, pltpu.roll(act, rows - 1, 0))
-        trio = [x.astype(jnp.bfloat16) for x in (above, act, below)]
+        act = act.astype(jnp.bfloat16)
         for g in range(4):
-            for di in range(3):
-                for a in range(F + 2):
-                    act3[g * 8 + k + 1, a, :, pl.ds(di * C, C)] = trio[di][
-                        g * wide + a * H : g * wide + (a + 1) * H
-                    ]
+            act_ref[pl.ds(g * 8 + k + 1, 1)] = act[g * wide : (g + 1) * wide].reshape(
+                1, F + 2, H, C
+            )
             for a in range(F):
                 hid[g * 8 + k, a] = h0[g * wide + (a + 2) * H : g * wide + (a + 3) * H]
         return carry
 
     lax.fori_loop(0, 8, columns, 0)
 
-    for dt in range(3):
-        for di in range(3):
-            for dj in range(3):
-                pltpu.make_async_copy(
-                    w_mid_ref.at[dt, di, dj],
-                    wmid.at[dt, pl.ds(dj * 3 * C + di * C, C)],
-                    wmid_sem.at[dt * 9 + di * 3 + dj],
-                ).wait()
+    for copy in mid_copies:
+        copy.wait()
 
     after = lax.rem(me + 1, n)
 
@@ -187,16 +191,23 @@
     def residual(m, carry):
         f = m // (W // CHUNK)
         w0 = pl.multiple_of(lax.rem(m, W // CHUNK) * CHUNK, CHUNK)
-        acc = hid[pl.ds(w0, CHUNK), f].astype(jnp.float32).reshape(CHUNK * H, C) + b_mid_ref[...]
-        for dt in range(3):
-            left = jnp.concatenate(
-                [
-                    act3[pl.ds(w0 + dj, CHUNK), f + dt].reshape(CHUNK * H, 3 * C)
-                    for dj in range(3)
-                ],
-                axis=1,
-            )
-            acc = acc + jnp.dot(left, wmid[dt], preferred_element_type=jnp.float32)
+        left = jnp.concatenate(
+            [
+                act_ref[pl.ds(w0 + dj, CHUNK), f + dt].reshape(CHUNK * H, C)
+                for dt in range(3)
+                for dj in range(3)
+            ],
+            axis=1,
+        )
+        three = jnp.dot(
+            left, wmid[...].reshape(9 * C, 3 * C), preferred_element_type=jnp.float32
+        )
+        row = lax.broadcasted_iota(jnp.int32, (CHUNK * H, C), 0) & (H - 1)
+        above = pltpu.roll(three[:, :C], 1, 0)
+        below = pltpu.roll(three[:, 2 * C :], CHUNK * H - 1, 0)
+        acc = hid[pl.ds(w0, CHUNK), f].astype(jnp.float32).reshape(CHUNK * H, C)
+        acc = acc + b_mid[...][None, :] + three[:, C : 2 * C]
+        acc = acc + jnp.where(row == 0, 0.0, above) + jnp.where(row == H - 1, 0.0, below)
         for c in range(C // 128):
             turn[c] = acc[:, c * 128 : (c + 1) * 128]
         for i in range(H):
@@ -230,7 +241,7 @@
         ]
         for f in range(F):
             left = jnp.concatenate(blocks[f : f + 3], axis=1)
-            up = jnp.dot(left, wtime[...], preferred_element_type=jnp.float32) + b_time_ref[...]
+            up = jnp.dot(left, wtime[...], preferred_element_type=jnp.float32) + b_time[...][None, :]
             up = up.astype(jnp.bfloat16)
             for s in range(2):
                 out_ref[2 * f + s, pl.ds(i0, 4)] = up[:, s * C : (s + 1) * C].reshape(4, W, C)
@@ -255,43 +266,46 @@
     assert frames == F * n
     bf16, f32 = jnp.bfloat16, jnp.float32
     vmem = pl.BlockSpec(memory_space=pltpu.VMEM)
-    hbm = pl.BlockSpec(memory_space=pl.ANY)
+    hbm = pl.BlockSpec(memory_space=pltpu.HBM)
     chunks = F * (W // CHUNK)
     dma = pltpu.SemaphoreType.DMA
     return pl.pallas_call(
         functools.partial(kernel, n),
         out_shape=jax.ShapeDtypeStruct((2 * F, H, W, C), bf16),
-        in_specs=[vmem, hbm, vmem, vmem, hbm, vmem, hbm, vmem],
+        in_specs=[hbm] * 8,
         out_specs=vmem,
         scratch_shapes=[
+            pltpu.VMEM((C,), f32), pltpu.VMEM((C,), f32), pltpu.VMEM((C,), f32),
+            pltpu.VMEM((2 * C,), f32),
+            pltpu.VMEM((frames, block), bf16),
             pltpu.VMEM((frames + 16, block), f32),
             pltpu.VMEM((n, 8, block), bf16),
             pltpu.VMEM((n, 8, block), bf16),
             pltpu.VMEM((block // 128, n * 8, 128), f32),
             pltpu.VMEM((2, 3, (F + 4) * H, WIDE), f32),
             pltpu.VMEM((10 * KT, C), bf16),
-            pltpu.VMEM((3, 9 * C, C), bf16),
+            pltpu.VMEM((3, 3, C, 3 * C), bf16),
             pltpu.VMEM((3 * C, 2 * C), bf16),
-            pltpu.VMEM((W + 2, F + 2, H, 3 * C), bf16),
+            pltpu.VMEM((W + 2, F + 2, H, C), bf16),
             pltpu.VMEM((W, F, H, C), bf16),
             pltpu.VMEM((C // 128, CHUNK * H, 128), f32),
             pltpu.VMEM((F, H, W, C), bf16),
             pltpu.VMEM((F, H, W, C), bf16),
-            dma((n,)), dma((n,)), dma((chunks,)), dma((chunks,)), dma((9,)), dma((27,)), dma(()),
+            dma((n,)), dma((n,)), dma((chunks,)), dma((chunks,)), dma((9,)), dma((9,)), dma(()), dma(()), dma((4,)),
         ],
         compiler_params=pltpu.CompilerParams(
-            collective_id=0, has_side_effects=True, vmem_limit_bytes=48 * 1024 * 1024
+            collective_id=0, has_side_effects=True, vmem_limit_bytes=64000000
         ),
         name="decoder_window",
     )(
         latent,
         w_in.reshape(9, 3 * ZC, C),
-        b_in.reshape(1, C),
-        gain.reshape(1, C),
+        b_in,
+        gain,
         w_mid,
-        b_mid.reshape(1, C),
+        b_mid,
         w_time.reshape(3 * C, 2 * C),
-        b_time.reshape(1, 2 * C),
+        b_time,
     )
 
 

time: 43.5 us -> 36.6 us (0.84)
  local copies, waits for them, and re-layouts: 7.09 us -> 2.74 us
  Pallas kernels: 36 us -> 33.7 us
    reshape x4 -> x0, local copies, waits for them, and re-layouts: 2.74 us -> none  [the longest x1 0.69 us: per_device(): b_time.reshape(1, 2 * C)]
    pallas_call x1, Pallas kernels: 36 us -> 33.7 us  [per_device(): pl.pallas_call(functools.partial(kernel, n), out_shape=jax.ShapeDtypeStru...]
    unnamed x7 -> x1, local copies, waits for them, and re-layouts: 4.35 us -> 2.74 us
where the time goes in v2:
time: 36.6 us; the launch traced here: 36.5 us
  Pallas kernels  33.7 us (92%)
  local copies, waits for them, and re-layouts  2.74 us (7%)
    pallas_call x1, Pallas kernels, per_device(): pl.pallas_call(functools.partial(kernel, n), out_shape=jax.ShapeDtypeStru...  33.7 us
    unnamed x1, local copies, waits for them, and re-layouts  2.74 us

profile of v2, /device:TPU:8, one launch (start us, length us, event | category | flops | bytes accessed | tf_op | source)
XLA Modules:
  0.0 36.5 jit_solution(5219837594092510849)
XLA Ops:
  0.0 33.7 %decoder_window.1 = bf16[4,16,32,384]{3,2,1,0:T(8,128)(2,1)} custom-call(bf16[32,512]{1,0:T(8,128)(2,1)} %latent_ref.1, bf16[9,48,384]{2,1,0:T(8,128)(2,1)} %bitcast.3, f32[384]{0:T(512)} %b_in_ref.1, f32[384]{0:T(512)} %gain_ref.1, bf16[3,3,3,384,384]{4,3,2,1,0:T(8,128)(2,1)} %w_mid_ref.1, f32[384]{0:T(512)} %b_mid_ref.1, bf16[1152,768]{1,0:T(8,128)(2,1)} %bitcast.2, ...), custom_call_target="tpu_custom_call" | custom-call | tf_op jit(solution)/shard_map/decoder_window/pallas_call | solution.py:272
  33.7 2.7 %copy.10 = bf16[4,16,32,384]{3,2,1,0:T(8,128)(2,1)} copy(bf16[4,16,32,384]{3,2,1,0:T(8,128)(2,1)} %decoder_window.1) | data formatting | bytes 3145728

commit v3 on v2

--- a/solution.py
+++ b/solution.py
@@ -22,7 +22,7 @@
 def kernel(
     n, latent_ref, w_in_ref, b_in_ref, gain_ref, w_mid_ref, b_mid_ref, w_time_ref, b_time_ref,
     out_ref,
-    b_in, gain, b_mid, b_time, mine, padded, sent, got, spread, shifted, win, wmid, wtime, act_ref, hid, turn, own, halo,
+    b_in, gain, b_mid, b_time, mine, padded, sent, got, spread, shifted, win, wmid, wtime, act_ref, hid, turn, part, own, halo,
     lat_send, lat_recv, halo_send, halo_recv, win_sem, wmid_sem, wtime_sem, mine_sem, vec_sem,
 ):
     me = lax.axis_index("tm")
@@ -225,6 +225,21 @@
 
     pltpu.make_async_copy(w_time_ref, wtime, wtime_sem).wait()
 
+    def upsample_own(q, carry):
+        mine0, mine1 = (own[f, pl.ds(q * 4, 4)].reshape(4 * W, C) for f in range(F))
+        here = pl.ds(q * 4 * W, 4 * W)
+        part[0, here] = jnp.dot(
+            mine0, wtime[pl.ds(2 * C, C)], preferred_element_type=jnp.float32
+        )
+        part[1, here] = jnp.dot(
+            jnp.concatenate([mine0, mine1], axis=1),
+            wtime[pl.ds(C, 2 * C)],
+            preferred_element_type=jnp.float32,
+        )
+        return carry
+
+    lax.fori_loop(0, H // 4, upsample_own, 0)
+
     @pl.when(me > 0)
     def _():
         for m in range(chunks):
@@ -236,12 +251,18 @@
 
     def upsample(q, carry):
         i0 = q * 4
-        blocks = [
-            (halo if f < 2 else own)[f % 2, pl.ds(i0, 4)].reshape(4 * W, C) for f in range(4)
-        ]
+        past0, past1 = (halo[f, pl.ds(i0, 4)].reshape(4 * W, C) for f in range(F))
+        here = pl.ds(q * 4 * W, 4 * W)
+        from_halo = (
+            jnp.dot(
+                jnp.concatenate([past0, past1], axis=1),
+                wtime[pl.ds(0, 2 * C)],
+                preferred_element_type=jnp.float32,
+            ),
+            jnp.dot(past1, wtime[pl.ds(0, C)], preferred_element_type=jnp.float32),
+        )
         for f in range(F):
-            left = jnp.concatenate(blocks[f : f + 3], axis=1)
-            up = jnp.dot(left, wtime[...], preferred_element_type=jnp.float32) + b_time[...][None, :]
+            up = from_halo[f] + part[f, here] + b_time[...][None, :]
             up = up.astype(jnp.bfloat16)
             for s in range(2):
                 out_ref[2 * f + s, pl.ds(i0, 4)] = up[:, s * C : (s + 1) * C].reshape(4, W, C)
@@ -289,6 +310,7 @@
             pltpu.VMEM((W + 2, F + 2, H, C), bf16),
             pltpu.VMEM((W, F, H, C), bf16),
             pltpu.VMEM((C // 128, CHUNK * H, 128), f32),
+            pltpu.VMEM((F, H * W, 2 * C), f32),
             pltpu.VMEM((F, H, W, C), bf16),
             pltpu.VMEM((F, H, W, C), bf16),
             dma((n,)), dma((n,)), dma((chunks,)), dma((chunks,)), dma((9,)), dma((9,)), dma(()), dma(()), dma((4,)),

time: 36.6 us -> 35.6 us (0.973)
  Pallas kernels: 33.7 us -> 32.7 us
    pallas_call x1, Pallas kernels: 33.7 us -> 32.7 us  [per_device(): pl.pallas_call(functools.partial(kernel, n), out_shape=jax.ShapeDtypeStru...]
where the time goes in v3:
time: 35.6 us; the launch traced here: 35.4 us
  Pallas kernels  32.7 us (92%)
  local copies, waits for them, and re-layouts  2.74 us (8%)
    pallas_call x1, Pallas kernels, per_device(): pl.pallas_call(functools.partial(kernel, n), out_shape=jax.ShapeDtypeStru...  32.7 us
    unnamed x1, local copies, waits for them, and re-layouts  2.74 us

profile of v3, /device:TPU:8, one launch (start us, length us, event | category | flops | bytes accessed | tf_op | source)
XLA Modules:
  0.0 35.4 jit_solution(9039917690081895953)
XLA Ops:
  0.0 32.7 %decoder_window.1 = bf16[4,16,32,384]{3,2,1,0:T(8,128)(2,1)} custom-call(bf16[32,512]{1,0:T(8,128)(2,1)} %latent_ref.1, bf16[9,48,384]{2,1,0:T(8,128)(2,1)} %bitcast.3, f32[384]{0:T(512)} %b_in_ref.1, f32[384]{0:T(512)} %gain_ref.1, bf16[3,3,3,384,384]{4,3,2,1,0:T(8,128)(2,1)} %w_mid_ref.1, f32[384]{0:T(512)} %b_mid_ref.1, bf16[1152,768]{1,0:T(8,128)(2,1)} %bitcast.2, ...), custom_call_target="tpu_custom_call" | custom-call | tf_op jit(solution)/shard_map/decoder_window/pallas_call | solution.py:293
  32.7 2.7 %copy.10 = bf16[4,16,32,384]{3,2,1,0:T(8,128)(2,1)} copy(bf16[4,16,32,384]{3,2,1,0:T(8,128)(2,1)} %decoder_window.1) | data formatting | bytes 3145728
